TPU v7x, 32 devices: a whole 2x2x4 slice. The times are simulated.
32 devices in a mesh: tile: 8 (over y, x, core), aux: 4 (over z).
Axes of the slice: x: 2, y: 2, z: 4, core: 2. Of those that a mesh axis runs over, the one named last changes fastest.
Arguments:
- amps: bfloat16 [8, 8, 128, 128], P('tile'), may hold values from -6 to 6
- fitted: bfloat16 [2048, 8, 128], P('aux'), may hold values from -0.375 to 0.375
- screen: int32 [16, 8], P('aux'), may hold values 0 or 1
- owner: int32 [8], replicated, may hold values from 0 to 7, each once
- eps_occ: float32 [8], replicated, may hold values from -2 to -0.5
- eps_vir: float32 [128], replicated, may hold values from 0.5 to 2
Outputs:
- update: bfloat16 [8, 128, 8, 128], P(None, None, 'tile')
Inputs may be any that keep to these rules, and one draw needn't show every extreme that they name: owner is a permutation of the occupied orbitals.
All inputs are finite; a program needn't handle non-finite values. No bound on the sum of `screen` on one device may be relied on, other than what follows from the above.
Results may differ from a plain program's by a relative error of at most 0.0034.
Values may be sent and summed in bfloat16 or wider, within the bound.
No kernel may reach another device: no remote copies, remote signals or barrier semaphores. Data moves between devices by JAX's collectives and lax.ppermute only.
A program may use at most 64 MiB of HBM per device.

v0:
```python
import jax
import jax.numpy as jnp
from jax import lax
from jax.sharding import PartitionSpec as P


def on_device(amps, fitted, screen, owner, eps_occ, eps_vir):
    occ_dev = amps.shape[0]
    qblock_size = fitted.shape[0] // screen.shape[0]
    tile_mask = jnp.repeat(screen, qblock_size, axis=0).astype(jnp.bfloat16)
    screened = fitted * tile_mask[:, :, None]
    permuted = jnp.take(amps, owner, axis=1)
    received = lax.all_to_all(permuted, "tile", split_axis=1, concat_axis=0, tiled=True)
    intermed = jnp.einsum(
        "qkc,kpcb->qpb", screened, received, preferred_element_type=jnp.float32
    ).astype(jnp.bfloat16)
    partial_cycle = jnp.einsum(
        "qia,qpb->iapb", screened, intermed, preferred_element_type=jnp.float32
    )
    slot_start = lax.axis_index("tile") * occ_dev
    own_owner = lax.dynamic_slice_in_dim(owner, slot_start, occ_dev, 0)
    eps_slot = jnp.take(eps_occ, own_owner, axis=0)
    virt_pair = (
        eps_vir[None, :, None, None] + eps_vir[None, None, None, :] - eps_slot[None, None, :, None]
    )
    occ_rows = partial_cycle.shape[0]
    aux_count = lax.axis_size("aux")
    share_rows = -(-occ_rows // aux_count)
    extra_rows = share_rows * aux_count - occ_rows
    padded = jnp.pad(partial_cycle, ((0, extra_rows), (0, 0), (0, 0), (0, 0)))
    cycle_share = lax.psum_scatter(padded, "aux", scatter_dimension=0, tiled=True)
    eps_padded = jnp.pad(eps_occ, (0, extra_rows))
    eps_share = lax.dynamic_slice_in_dim(
        eps_padded, lax.axis_index("aux") * share_rows, share_rows, 0
    )
    denominator = virt_pair - eps_share[:, None, None, None]
    divided = (cycle_share / denominator).astype(jnp.bfloat16)
    gathered = lax.all_gather(divided, "aux", axis=0, tiled=True)
    return gathered[:occ_rows]


def solution(mesh):
    placed = (P("tile", None, None, None), P("aux", None, None), P("aux", None), P(), P(), P())
    return jax.shard_map(
        on_device,
        mesh=mesh,
        in_specs=placed,
        out_specs=P(None, None, "tile", None),
        check_vma=False,
    )
```

profile of v0, /device:TPU:0, one launch (start us, length us, event | category | flops | bytes accessed | tf_op | source)
XLA Modules:
  0.0 68.3 jit_solution(11172948436916942346)
XLA Ops:
  6.5 0.0 copy-start
  6.5 0.0 copy-start.4
  6.5 0.0 copy-start.1
  6.5 0.8 %compare_select_fusion = s32[8]{0:T(128)S(1)} fusion(s32[8]{0:T(128)} %param.9), kind=kLoop, calls=%fused_computation.12 | loop fusion | flops 24 | bytes 64 | tf_op jit(solution)/shard_map/jit(_take)/jit(_where)/select_n | solution.py:12
  7.3 0.0 copy-done.4
  7.3 0.2 copy-done
  7.5 0.6 gather_fusion
  8.1 0.8 %bitcast_select_fusion = bf16[1,8,128,128]{3,2,0,1:T(8,128)(2,1)} fusion(bf16[8,128,128]{2,1,0:T(8,128)(2,1)S(1)} %gather_fusion, pred[8]{0:T(512)(128)(4,1)S(1)} %compare_and_fusion), kind=kLoop, calls=%fused_computation.7 | loop fusion | flops 131072 | bytes 524296 | tf_op jit(solution)/shard_map/jit(_take)/select_n | solution.py:12
  8.9 0.0 copy-start.3
  8.9 5.3 %all-to-all-start = ((bf16[1,8,128,128]{3,2,0,1:T(8,128)(2,1)}), bf16[1,8,128,128]{3,2,0,1:T(8,128)(2,1)}, u32[]{:S(2)}, u32[]{:S(2)}) async-start(bf16[1,8,128,128]{3,2,0,1:T(8,128)(2,1)} %bitcast_select_fusion), calls=%async_computation | async-start | bytes 524288 | tf_op jit(solution)/shard_map/all_to_all | solution.py:13
  14.2 0.0 reduce-scatter.2.cloned.1.call-start
  14.3 0.0 copy-done.3
  14.3 0.0 copy-done.1
  14.3 0.7 %broadcast_multiply_fusion = bf16[512,8,128]{2,1,0:T(8,128)(2,1)S(1)} fusion(bf16[512,8,128]{2,1,0:T(8,128)(2,1)S(1)} %copy-done.1, bf16[512,8]{1,0:T(8,128)(2,1)S(1)} %bitcast.29), kind=kLoop, calls=%fused_computation.5 | loop fusion | flops 524288 | bytes 2105344 | tf_op jit(solution)/shard_map/mul | solution.py:11
  15.1 0.7 copy.9
  15.7 5.5 %all-to-all-done = bf16[1,8,128,128]{3,2,0,1:T(8,128)(2,1)} async-done(((bf16[1,8,128,128]{3,2,0,1:T(8,128)(2,1)}), bf16[1,8,128,128]{3,2,0,1:T(8,128)(2,1)}, u32[]{:S(2)}, u32[]{:S(2)}) %all-to-all-start) | async-done | bytes 262176 | tf_op jit(solution)/shard_map/all_to_all | solution.py:13
  21.2 3.1 %convolution_bitcast_fusion = f32[8,128,1,128]{3,1,0,2:T(8,128)} fusion(bf16[512,8,128]{0,2,1:T(8,128)(2,1)S(1)} %copy.9, bf16[1,8,128,128]{3,2,0,1:T(8,128)(2,1)} %all-to-all-done), kind=kOutput, calls=%fused_computation.1 | convolution fusion | flops 268500992 | bytes 1835008 | tf_op jit(solution)/shard_map/qia,qpb->iapb/dot_general | solution.py:17
  24.3 0.0 reduce-scatter.2.cloned.1.call-update
  24.3 0.6 dynamic_slice.6
  26.9 0.0 copy-start.5
  26.9 0.6 copy-done.5
  27.5 0.1 dynamic_slice.7
  27.6 0.6 dynamic-slice.2
  28.7 0.0 copy-start.2
  28.7 0.6 copy-done.2
  29.4 0.1 add_subtract_fusion
  29.4 16.5 %reduce-scatter.2.cloned.1.call-done = f32[2,128,1,128]{3,1,0,2:T(8,128)} async-done(((f32[8,128,1,128]{3,1,0,2:T(8,128)}), f32[2,128,1,128]{3,1,0,2:T(8,128)}) %reduce-scatter.2.cloned.1.call-update) | async-done | bytes 131088 | tf_op jit(solution)/shard_map/reduce_scatter | solution.py:31
  45.9 1.0 %fusion.4 = bf16[2,128,1,128]{3,1,2,0:T(8,128)(2,1)S(1)} fusion(f32[2,128,1,128]{3,1,0,2:T(8,128)} %reduce-scatter.2.cloned.1.call-done, f32[2]{0:T(128)S(1)} %dynamic_slice.7, f32[128,128]{1,0:T(8,128)S(1)} %add_subtract_fusion), kind=kLoop, calls=%fused_computation.10 | loop fusion | flops 98304 | bytes 262152 | tf_op jit(solution)/shard_map/convert_element_type | solution.py:37
  46.9 13.8 %all_gather.3 = bf16[8,128,1,128]{3,1,2,0:T(8,128)(2,1)S(1)} all-gather(bf16[2,128,1,128]{3,1,2,0:T(8,128)(2,1)S(1)} %fusion.4), channel_id=1, replica_groups=mesh['tile'=8,'aux'=4] {'aux'}, dimensions={0}, use_global_device_ids=true | all-gather | bytes 327680 | tf_op jit(solution)/shard_map/all_gather | solution.py:38
  60.7 0.7 %copy.13 = bf16[8,128,1,128]{3,1,2,0:T(8,128)(2,1)} copy(bf16[8,128,1,128]{3,1,2,0:T(8,128)(2,1)S(1)} %all_gather.3) | data formatting | bytes 524288
  (4 shorter events, 0.0 us)
Async XLA Ops:
  6.5 1.0 %copy-start = (bf16[1,8,128,128]{3,2,1,0:T(8,128)(2,1)S(1)}, bf16[1,8,128,128]{3,2,1,0:T(8,128)(2,1)}, u32[]{:S(2)}) copy-start(bf16[1,8,128,128]{3,2,1,0:T(8,128)(2,1)} %param.6) | copy-start | bytes 786436
  6.5 0.8 %copy-start.4 = (s32[8]{0:T(128)S(1)}, s32[8]{0:T(128)}, u32[]{:S(2)}) copy-start(s32[8]{0:T(128)} %param.9) | copy-start | bytes 100
  6.5 7.8 %copy-start.1 = (bf16[512,8,128]{2,1,0:T(8,128)(2,1)S(1)}, bf16[512,8,128]{2,1,0:T(8,128)(2,1)}, u32[]{:S(2)}) copy-start(bf16[512,8,128]{2,1,0:T(8,128)(2,1)} %param.7) | copy-start | bytes 3145732
  8.9 5.4 %copy-start.3 = (s32[4,8]{1,0:T(4,128)S(1)}, s32[4,8]{1,0:T(4,128)}, u32[]{:S(2)}) copy-start(s32[4,8]{1,0:T(4,128)} %param.8) | copy-start | bytes 388
  8.9 12.3 %all-to-all-start = ((bf16[1,8,128,128]{3,2,0,1:T(8,128)(2,1)}), bf16[1,8,128,128]{3,2,0,1:T(8,128)(2,1)}, u32[]{:S(2)}, u32[]{:S(2)}) async-start(bf16[1,8,128,128]{3,2,0,1:T(8,128)(2,1)} %bitcast_select_fusion), calls=%async_computation | async-start | bytes 524288 | tf_op jit(solution)/shard_map/all_to_all | solution.py:13
  14.2 31.7 %reduce-scatter.2.cloned.1.call-start = ((), (), s32[]{:S(2)}) async-start(), calls=%async_computation.2 | async-start | bytes 655360 | tf_op jit(solution)/shard_map/reduce_scatter | solution.py:31
  26.9 0.7 copy-start.5
  28.7 0.7 copy-start.2
Sparse Core Ops, SparseCore 0:
  24.4 21.4 reduce-scatter.1
where the time goes:
time: 68.6 us; the launch traced here: 68.3 us
  waiting for transfers between devices  22 us (32%)
  between operations  16 us (23%)
  blocking collectives  13.8 us (20%)
  starting transfers between devices  5.37 us (8%)
  local copies, waits for them, and re-layouts  4.7 us (7%)
  other arithmetic  3.36 us (5%)
  matrix products  3.05 us (4%)
    reduce_scatter x1, waiting for transfers between devices, on_device(): lax.psum_scatter(padded, 'aux', scatter_dimension=0, tiled=True)  16.5 us
    all_gather x1, blocking collectives, on_device(): gathered = lax.all_gather(divided, 'aux', axis=0, tiled=True)  13.8 us
    all_to_all x1, waiting for transfers between devices, on_device(): lax.all_to_all(permuted, 'tile', split_axis=1, concat_axis=0, tiled=True)  5.5 us
    all_to_all x1, starting transfers between devices, on_device(): lax.all_to_all(permuted, 'tile', split_axis=1, concat_axis=0, tiled=True)  5.33 us
    dot_general x1, matrix products, on_device(): jnp.einsum('qia,qpb->iapb', screened, intermed, preferred_element_type=jn...  3.05 us
    unnamed x13, local copies, waits for them, and re-layouts  2.19 us
    select_n x2, other arithmetic, on_device(): permuted = jnp.take(amps, owner, axis=1)  1.56 us
  transfers between devices with their start and end apart: 2, of which 2 were waited for; matrix products, arithmetic and copies ran while one was open for 4% of the time, Pallas kernels for 0%

commit v1 on v0

--- a/solution.py
+++ b/solution.py
@@ -2,6 +2,24 @@
 import jax.numpy as jnp
 from jax import lax
 from jax.sharding import PartitionSpec as P
+
+
+def joined_along(blocks, dim):
+    blocks = jnp.moveaxis(blocks, 0, dim)
+    dims = blocks.shape
+    return blocks.reshape(*dims[:dim], dims[dim] * dims[dim + 1], *dims[dim + 2 :])
+
+
+def collected_by_bits(shard, axis):
+    size = lax.axis_size(axis)
+    blocks = shard[None]
+    for level in range(size.bit_length() - 1):
+        bit = 1 << level
+        theirs = lax.ppermute(blocks, axis, [(i, i ^ bit) for i in range(size)])
+        both = jnp.stack([blocks, theirs])
+        upper = lax.axis_index(axis) >> level & 1
+        blocks = jnp.where(upper == 0, both, both[::-1]).reshape(-1, *shard.shape)
+    return blocks
 
 
 def on_device(amps, fitted, screen, owner, eps_occ, eps_vir):
@@ -35,7 +53,7 @@
     )
     denominator = virt_pair - eps_share[:, None, None, None]
     divided = (cycle_share / denominator).astype(jnp.bfloat16)
-    gathered = lax.all_gather(divided, "aux", axis=0, tiled=True)
+    gathered = joined_along(collected_by_bits(divided, "aux"), 0)
     return gathered[:occ_rows]
 
 

time: 68.6 us -> 66.2 us (0.965)
  blocking collectives: 13.8 us -> 0 us
  waiting for transfers between devices: 22 us -> 32 us
  other arithmetic: 3.36 us -> 4.37 us
  starting transfers between devices: 5.37 us -> 6.24 us
    all_gather x1 -> x0, blocking collectives: 13.8 us -> none  [on_device(): gathered = lax.all_gather(divided, 'aux', axis=0, tiled=True)]
    ppermute x0 -> x2, waiting for transfers between devices: none -> 10.1 us  [collected_by_bits(): theirs = lax.ppermute(blocks, axis, [(i, i ^ bit) for i in range(size)])]
    broadcast_in_dim x0 -> x1, other arithmetic: none -> 1.07 us  [collected_by_bits(): blocks = shard[None]]
    convert_element_type x1 -> x0, other arithmetic: 1 us -> none  [on_device(): divided = (cycle_share / denominator).astype(jnp.bfloat16)]
    ppermute x0 -> x2, starting transfers between devices: none -> 0.87 us  [collected_by_bits(): theirs = lax.ppermute(blocks, axis, [(i, i ^ bit) for i in range(size)])]
    select_n x0 -> x1, other arithmetic: none -> 0.76 us  [collected_by_bits(): blocks = jnp.where(upper == 0, both, both[::-1]).reshape(-1, *shard.shape)]
    unnamed x13 -> x14, local copies, waits for them, and re-layouts: 2.19 us -> 1.49 us
  transfers between devices with their start and end apart: 2 -> 4, of which waited for: 2 -> 4; matrix products, arithmetic and copies ran while one was open for 4% -> 4% of each run, Pallas kernels for 0% -> 0%
where the time goes in v1:
time: 66.2 us; the launch traced here: 65.8 us
  waiting for transfers between devices  32 us (48%)
  between operations  16.1 us (24%)
  starting transfers between devices  6.24 us (9%)
  other arithmetic  4.37 us (7%)
  local copies, waits for them, and re-layouts  4.08 us (6%)
  matrix products  3.05 us (5%)
    reduce_scatter x1, waiting for transfers between devices, on_device(): lax.psum_scatter(padded, 'aux', scatter_dimension=0, tiled=True)  16.3 us
    ppermute x2, waiting for transfers between devices, collected_by_bits(): theirs = lax.ppermute(blocks, axis, [(i, i ^ bit) for i in range(size)])  10.1 us
    all_to_all x1, waiting for transfers between devices, on_device(): lax.all_to_all(permuted, 'tile', split_axis=1, concat_axis=0, tiled=True)  5.5 us
    all_to_all x1, starting transfers between devices, on_device(): lax.all_to_all(permuted, 'tile', split_axis=1, concat_axis=0, tiled=True)  5.33 us
    dot_general x1, matrix products, on_device(): jnp.einsum('qia,qpb->iapb', screened, intermed, preferred_element_type=jn...  3.05 us
    select_n x2, other arithmetic, on_device(): permuted = jnp.take(amps, owner, axis=1)  1.56 us
    unnamed x14, local copies, waits for them, and re-layouts  1.49 us
  transfers between devices with their start and end apart: 4, of which 4 were waited for; matrix products, arithmetic and copies ran while one was open for 4% of the time, Pallas kernels for 0%

profile of v1, /device:TPU:0, one launch (start us, length us, event | category | flops | bytes accessed | tf_op | source)
XLA Modules:
  0.0 65.8 jit_solution(2126069452990933894)
XLA Ops:
  6.5 0.0 copy-start
  6.5 0.8 %compare_select_fusion = s32[8]{0:T(128)S(1)} fusion(s32[8]{0:T(128)} %param.9), kind=kLoop, calls=%fused_computation.17 | loop fusion | flops 24 | bytes 64 | tf_op jit(solution)/shard_map/jit(_take)/jit(_where)/select_n | solution.py:30
  7.3 0.0 copy-done.5
  7.3 0.2 copy-done
  7.5 0.6 gather_fusion
  8.1 0.8 %bitcast_select_fusion = bf16[1,8,128,128]{3,2,0,1:T(8,128)(2,1)} fusion(bf16[8,128,128]{2,1,0:T(8,128)(2,1)S(1)} %gather_fusion, pred[8]{0:T(512)(128)(4,1)S(1)} %compare_and_fusion), kind=kLoop, calls=%fused_computation.9 | loop fusion | flops 131072 | bytes 524296 | tf_op jit(solution)/shard_map/jit(_take)/select_n | solution.py:30
  8.9 5.3 %all-to-all-start = ((bf16[1,8,128,128]{3,2,0,1:T(8,128)(2,1)}), bf16[1,8,128,128]{3,2,0,1:T(8,128)(2,1)}, u32[]{:S(2)}, u32[]{:S(2)}) async-start(bf16[1,8,128,128]{3,2,0,1:T(8,128)(2,1)} %bitcast_select_fusion), calls=%async_computation | async-start | bytes 524288 | tf_op jit(solution)/shard_map/all_to_all | solution.py:31
  14.2 0.0 reduce-scatter.2.cloned.1.call-start
  14.3 0.0 copy-done.4
  14.3 0.0 copy-done.1
  14.3 0.7 %broadcast_multiply_fusion = bf16[512,8,128]{2,1,0:T(8,128)(2,1)S(1)} fusion(bf16[512,8,128]{2,1,0:T(8,128)(2,1)S(1)} %copy-done.1, bf16[512,8]{1,0:T(8,128)(2,1)S(1)} %bitcast.40), kind=kLoop, calls=%fused_computation.5 | loop fusion | flops 524288 | bytes 2105344 | tf_op jit(solution)/shard_map/mul | solution.py:29
  15.1 0.7 %copy.9 = bf16[512,8,128]{0,2,1:T(8,128)(2,1)S(1)} copy(bf16[512,8,128]{2,1,0:T(8,128)(2,1)S(1)} %broadcast_multiply_fusion) | data formatting | bytes 2097152 | tf_op jit(solution)/shard_map/mul | solution.py:29
  15.7 5.5 %all-to-all-done = bf16[1,8,128,128]{3,2,0,1:T(8,128)(2,1)} async-done(((bf16[1,8,128,128]{3,2,0,1:T(8,128)(2,1)}), bf16[1,8,128,128]{3,2,0,1:T(8,128)(2,1)}, u32[]{:S(2)}, u32[]{:S(2)}) %all-to-all-start) | async-done | bytes 262176 | tf_op jit(solution)/shard_map/all_to_all | solution.py:31
  21.2 3.1 %convolution_bitcast_fusion = f32[8,128,1,128]{3,1,0,2:T(8,128)} fusion(bf16[512,8,128]{0,2,1:T(8,128)(2,1)S(1)} %copy.9, bf16[1,8,128,128]{3,2,0,1:T(8,128)(2,1)} %all-to-all-done), kind=kOutput, calls=%fused_computation.1 | convolution fusion | flops 268500992 | bytes 1835008 | tf_op jit(solution)/shard_map/qia,qpb->iapb/dot_general | solution.py:35
  24.3 0.0 reduce-scatter.2.cloned.1.call-update
  24.3 0.6 dynamic_slice.6
  26.9 0.0 copy-start.6
  26.9 0.6 copy-done.6
  27.5 0.1 dynamic_slice.7
  27.6 0.6 dynamic-slice.2
  28.9 0.0 copy-start.3
  28.9 0.6 copy-done.3
  29.5 0.1 add_subtract_fusion
  29.6 16.3 %reduce-scatter.2.cloned.1.call-done = f32[2,128,1,128]{3,1,0,2:T(8,128)} async-done(((f32[8,128,1,128]{3,1,0,2:T(8,128)}), f32[2,128,1,128]{3,1,0,2:T(8,128)}) %reduce-scatter.2.cloned.1.call-update) | async-done | bytes 131088 | tf_op jit(solution)/shard_map/reduce_scatter | solution.py:49
  45.9 1.1 %fusion.9 = bf16[1,2,128,1,128]{4,2,1,3,0:T(8,128)(2,1)S(1)} fusion(f32[2,128,1,128]{3,1,0,2:T(8,128)} %reduce-scatter.2.cloned.1.call-done, f32[2]{0:T(128)S(1)} %dynamic_slice.7, f32[128,128]{1,0:T(8,128)S(1)} %add_subtract_fusion), kind=kLoop, calls=%fused_computation.20 | loop fusion | flops 98304 | bytes 262152 | tf_op jit(solution)/shard_map/broadcast_in_dim | solution.py:15
  47.0 0.1 collective-permute-start
  47.1 0.0 copy-done.2
  47.1 0.1 fusion.8
  47.2 4.1 %collective-permute-done = bf16[1,2,128,1,128]{4,2,1,3,0:T(8,128)(2,1)S(1)} collective-permute-done((bf16[1,2,128,1,128]{4,2,1,3,0:T(8,128)(2,1)S(1)}, bf16[1,2,128,1,128]{4,2,1,3,0:T(8,128)(2,1)S(1)}, u32[]{:S(2)}, u32[]{:S(2)}) %collective-permute-start) | collective-permute-done | bytes 65568 | tf_op jit(solution)/shard_map/ppermute | solution.py:18
  51.4 0.8 %collective-permute-start.1 = (bf16[2,2,128,1,128]{4,2,1,0,3:T(8,128)(2,1)S(1)}, bf16[2,2,128,1,128]{4,2,1,0,3:T(8,128)(2,1)S(1)}, u32[]{:S(2)}, u32[]{:S(2)}) collective-permute-start(bf16[2,2,128,1,128]{4,2,1,0,3:T(8,128)(2,1)S(1)} %get-tuple-element.17), channel_id=1, source_target_pairs={{0,2},{1,3},{2,0},{3,1},{4,6},{5,7},{6,4},{7,5},{8,10},{9,11},{10,... | collective-permute-start | bytes 393224 | tf_op jit(solution)/shard_map/ppermute | solution.py:18
  52.2 6.0 %collective-permute-done.1 = bf16[2,2,128,1,128]{4,2,1,0,3:T(8,128)(2,1)S(1)} collective-permute-done((bf16[2,2,128,1,128]{4,2,1,0,3:T(8,128)(2,1)S(1)}, bf16[2,2,128,1,128]{4,2,1,0,3:T(8,128)(2,1)S(1)}, u32[]{:S(2)}, u32[]{:S(2)}) %collective-permute-start.1) | collective-permute-done | bytes 131104 | tf_op jit(solution)/shard_map/ppermute | solution.py:18
  58.2 0.8 %reverse_select_fusion = bf16[2,2,2,128,1,128]{5,3,2,1,4,0:T(8,128)(2,1)} fusion(bf16[2,2,2,128,1,128]{5,3,2,1,4,0:T(8,128)(2,1)S(1)} %pad_maximum_fusion, pred[]{:T(512)S(6)} %eq.6), kind=kLoop, calls=%fused_computation.6 | loop fusion | flops 131072 | bytes 524289 | tf_op jit(solution)/shard_map/jit(_where)/select_n | solution.py:21
  (11 shorter events, 0.1 us)
Async XLA Ops:
  6.5 1.0 %copy-start = (bf16[1,8,128,128]{3,2,1,0:T(8,128)(2,1)S(1)}, bf16[1,8,128,128]{3,2,1,0:T(8,128)(2,1)}, u32[]{:S(2)}) copy-start(bf16[1,8,128,128]{3,2,1,0:T(8,128)(2,1)} %param.6) | copy-start | bytes 786436
  6.5 0.8 %copy-start.5 = (s32[8]{0:T(128)S(1)}, s32[8]{0:T(128)}, u32[]{:S(2)}) copy-start(s32[8]{0:T(128)} %param.9) | copy-start | bytes 100
  6.5 7.8 %copy-start.1 = (bf16[512,8,128]{2,1,0:T(8,128)(2,1)S(1)}, bf16[512,8,128]{2,1,0:T(8,128)(2,1)}, u32[]{:S(2)}) copy-start(bf16[512,8,128]{2,1,0:T(8,128)(2,1)} %param.7) | copy-start | bytes 3145732
  8.9 5.4 %copy-start.4 = (s32[4,8]{1,0:T(4,128)S(1)}, s32[4,8]{1,0:T(4,128)}, u32[]{:S(2)}) copy-start(s32[4,8]{1,0:T(4,128)} %param.8) | copy-start | bytes 388
  8.9 12.3 %all-to-all-start = ((bf16[1,8,128,128]{3,2,0,1:T(8,128)(2,1)}), bf16[1,8,128,128]{3,2,0,1:T(8,128)(2,1)}, u32[]{:S(2)}, u32[]{:S(2)}) async-start(bf16[1,8,128,128]{3,2,0,1:T(8,128)(2,1)} %bitcast_select_fusion), calls=%async_computation | async-start | bytes 524288 | tf_op jit(solution)/shard_map/all_to_all | solution.py:31
  14.2 31.7 %reduce-scatter.2.cloned.1.call-start = ((), (), s32[]{:S(2)}) async-start(), calls=%async_computation.2 | async-start | bytes 655360 | tf_op jit(solution)/shard_map/reduce_scatter | solution.py:49
  26.9 0.7 %copy-start.6 = (f32[8]{0:T(128)S(1)}, f32[8]{0:T(128)}, u32[]{:S(2)}) copy-start(f32[8]{0:T(128)} %param.10) | copy-start | bytes 100
  28.9 0.7 %copy-start.3 = (f32[128]{0:T(128)S(1)}, f32[128]{0:T(128)}, u32[]{:S(2)}) copy-start(f32[128]{0:T(128)} %param.11) | copy-start | bytes 1540
  45.9 1.2 %copy-start.2 = (f32[2,128,1,128]{3,1,0,2:T(8,128)S(1)}, f32[2,128,1,128]{3,1,0,2:T(8,128)}, u32[]{:S(2)}) copy-start(f32[2,128,1,128]{3,1,0,2:T(8,128)} %reduce-scatter.2.cloned.1.call-done) | copy-start | bytes 393220
  47.0 4.3 %collective-permute-start = (bf16[1,2,128,1,128]{4,2,1,3,0:T(8,128)(2,1)S(1)}, bf16[1,2,128,1,128]{4,2,1,3,0:T(8,128)(2,1)S(1)}, u32[]{:S(2)}, u32[]{:S(2)}) collective-permute-start(bf16[1,2,128,1,128]{4,2,1,3,0:T(8,128)(2,1)S(1)} %fusion.9), channel_id=1, source_target_pairs={{0,1},{1,0},{2,3},{3,2},{4,5},{5,4},{6,7},{7,6},{8,9},{9,8},{10,11... | collective-permute-start | bytes 196616 | tf_op jit(solution)/shard_map/ppermute | solution.py:18
  51.4 6.8 %collective-permute-start.1 = (bf16[2,2,128,1,128]{4,2,1,0,3:T(8,128)(2,1)S(1)}, bf16[2,2,128,1,128]{4,2,1,0,3:T(8,128)(2,1)S(1)}, u32[]{:S(2)}, u32[]{:S(2)}) collective-permute-start(bf16[2,2,128,1,128]{4,2,1,0,3:T(8,128)(2,1)S(1)} %get-tuple-element.17), channel_id=1, source_target_pairs={{0,2},{1,3},{2,0},{3,1},{4,6},{5,7},{6,4},{7,5},{8,10},{9,11},{10,... | collective-permute-start | bytes 393224 | tf_op jit(solution)/shard_map/ppermute | solution.py:18
Sparse Core Ops, SparseCore 0:
  24.4 21.4 reduce-scatter.1
